TPU v7x, 32 devices: a whole 2x2x4 slice. The times are simulated.
32 devices in a mesh: groups: 2 (over y), row: 8 (over z, x), col: 2 (over core).
Axes of the slice: x: 2, y: 2, z: 4, core: 2. Of those that a mesh axis runs over, the one named last changes fastest.
Arguments:
- gram_old: bfloat16 [28672, 14336], P(('groups', 'row'), 'col'), parts along dimension 0, may hold values from -10 to 256, as said below
- activations: bfloat16 [256, 14336], P('groups', 'row'), parts along dimension 0, may hold values from -0.5 to 0.5
- weights: float32 [14336, 512], P('row', ('groups', 'col')), parts along dimension 1, may hold values from -6 to 6
- block_mask: int32 [112, 4], P(None, 'groups'), parts along dimension 1, may hold values 0 or 1
Outputs:
- pruned: float32 [14336, 512], P('row', ('groups', 'col')), parts along dimension 1
There are 2 independent parts, one for each index of `groups`. A program takes and returns all parts, laid end to end along the dimension named above; each array names one. Nothing has to cross between parts.
Inputs may be any that keep to these rules, and one draw needn't show every extreme that they name: `gram_old`: symmetric and positive definite.
All inputs are finite; a program needn't handle non-finite values.
Results may differ from a plain program's by a relative error of at most 0.00076.
Values may be sent and summed in bfloat16 or wider, within the bound.
A program may use at most 128 MiB of HBM per device.

v0:
```python
import jax
import jax.numpy as jnp
from jax import lax
from jax.sharding import PartitionSpec as P

K = 14336
BLK = 128
damping_ratio = 0.3
epsilon = 1e-06


def partner(value, axis, distance):
    return lax.ppermute(value, axis, [(i, i ^ 1 << distance) for i in range(lax.axis_size(axis))])


def expand_local(block_mask, row_offset, row_count, col_offset, col_count):
    row_ids = (row_offset + jnp.arange(row_count, dtype=jnp.int32)) // BLK
    col_ids = (col_offset + jnp.arange(col_count, dtype=jnp.int32)) // BLK
    pick_rows = (
        row_ids[:, None] == jnp.arange(block_mask.shape[0], dtype=jnp.int32)[None, :]
    ).astype(jnp.float32)
    pick_cols = (
        col_ids[:, None] == jnp.arange(block_mask.shape[1], dtype=jnp.int32)[None, :]
    ).astype(jnp.float32)
    partial_rows = jnp.dot(
        pick_rows, block_mask.astype(jnp.float32), precision=lax.Precision.HIGHEST
    )
    return jnp.dot(partial_rows, pick_cols.T, precision=lax.Precision.HIGHEST)


def update_product(activations, inner):
    high = inner.astype(jnp.bfloat16)
    low = (inner - high.astype(jnp.float32)).astype(jnp.bfloat16)
    contract = (((0,), (0,)), ((), ()))
    return lax.dot_general(
        activations, high, contract, preferred_element_type=jnp.float32
    ) + lax.dot_general(activations, low, contract, preferred_element_type=jnp.float32)


def per_device(gram_old, activations, weights, block_mask):
    row_block = gram_old.shape[0]
    half_width = gram_old.shape[1]
    width_cols = weights.shape[1]
    row_index = lax.axis_index("row")
    col_index = lax.axis_index("col")
    row_offset = row_index * row_block
    half_offset = col_index * half_width
    diag_column = row_offset + jnp.arange(row_block, dtype=jnp.int32) - half_offset
    on_diagonal = jnp.arange(half_width, dtype=jnp.int32)[None, :] == diag_column[:, None]
    trace_part = jnp.sum(jnp.where(on_diagonal, gram_old.astype(jnp.float32), 0.0))
    acts_wide = activations.astype(jnp.float32)
    trace_part = trace_part + jnp.sum(acts_wide * acts_wide) / lax.axis_size("col")
    mask_local = expand_local(block_mask, row_offset, row_block, col_index * width_cols, width_cols)

    def apply_gram(panel):
        panel_low = panel.astype(jnp.bfloat16)
        inner = lax.psum(jnp.dot(activations, panel_low, preferred_element_type=jnp.float32), "row")
        low_rank = update_product(activations, inner)
        column_panel = lax.all_gather(panel_low, "row", axis=0, tiled=True)
        own_half = lax.dynamic_slice_in_dim(column_panel, half_offset, half_width, 0)
        partner_need = lax.dynamic_slice_in_dim(
            column_panel, (1 - col_index) * half_width, half_width, 0
        )
        partner_half = partner(partner_need, "col", 0)
        own_part = jnp.dot(gram_old, own_half, preferred_element_type=jnp.float32)
        partner_part = jnp.dot(gram_old, partner_half, preferred_element_type=jnp.float32)
        return own_part + partner(partner_part, "col", 0) + low_rank

    kept_weights = mask_local * weights
    pruned_diff = kept_weights - weights
    grad_first = apply_gram(pruned_diff)
    step_dir = mask_local * grad_first
    curvature = apply_gram(step_dir)
    masked_curve = mask_local * curvature
    local_square = jnp.sum(step_dir * step_dir)
    local_curve = jnp.sum(step_dir * curvature)
    local_curve_square = jnp.sum(masked_curve * masked_curve)
    grad_square, grad_curve, curve_square, trace_total = lax.psum(
        jnp.stack([local_square, local_curve, local_curve_square, trace_part]), ("row", "col")
    )
    damping = damping_ratio * trace_total / K
    step_first = grad_square / (grad_curve + damping * grad_square + epsilon)
    step_second = (grad_curve + damping * grad_square) / (
        curve_square + 2.0 * damping * grad_curve + damping * damping * grad_square + epsilon
    )
    grad_second = grad_first - step_first * curvature
    return kept_weights - step_first * step_dir - step_second * (mask_local * grad_second)


def solution(mesh):
    placed = (
        P(("groups", "row"), "col"),
        P("groups", "row"),
        P("row", ("groups", "col")),
        P(None, "groups"),
    )
    return jax.shard_map(
        per_device,
        mesh=mesh,
        in_specs=placed,
        out_specs=P("row", ("groups", "col")),
        check_vma=False,
    )
```

profile of v0, /device:TPU:0, one launch (start us, length us, event | category | flops | bytes accessed | tf_op | source)
XLA Modules:
  0.0 419.9 jit_solution(6358814029816759565)
XLA Ops:
  6.6 2.0 fusion.4
  8.6 2.9 subtract_convert_fusion
  11.6 69.0 %all-gather.3.cloned.1.call-done = bf16[14336,128]{1,0:T(8,128)(2,1)} async-done(((bf16[1792,128]{1,0:T(8,128)(2,1)}), bf16[14336,128]{1,0:T(8,128)(2,1)}) %all-gather.3.cloned.1.call-update) | async-done | bytes 3670032 | tf_op jit(solution)/shard_map/all_gather | solution.py:59
  80.7 2.9 constant_dynamic-slice_fusion.1
  83.5 0.9 convolution_bitcast_fusion.5
  84.6 68.2 %all-reduce.3.cloned.1.call-done = f32[128,128]{0,1:T(8,128)} async-done(((f32[128,128]{0,1:T(8,128)}), f32[128,128]{0,1:T(8,128)}) %all-reduce.3.cloned.1.call-update) | async-done | bytes 65552 | tf_op jit(solution)/shard_map/psum | solution.py:57
  152.8 1.2 fusion.12
  154.0 12.5 %convolution_bitcast_fusion.2 = f32[1792,128]{1,0:T(8,128)S(1)} fusion(bf16[1792,7168]{1,0:T(8,128)(2,1)} %param.4, bf16[7168,128]{1,0:T(8,128)(2,1)} %collective-permute-done), kind=kOutput, calls=%fused_computation.6 | convolution fusion | flops 3288334336 | bytes 28442624 | tf_op jit(solution)/shard_map/dot_general | solution.py:66
  166.5 11.8 %convolution_bitcast_fusion.3 = f32[1792,128]{1,0:T(8,128)S(1)} fusion(bf16[1792,7168]{1,0:T(8,128)(2,1)} %param.4, bf16[14336,128]{1,0:T(8,128)(2,1)S(1)} %copy-done.4, s32[]{:T(128)S(6)} %select_n.32), kind=kOutput, calls=%fused_computation.7 | convolution fusion | flops 3288334336 | bytes 28442628 | tf_op jit(solution)/shard_map/dot_general | solution.py:65
  178.4 1.8 fusion.24
  180.5 66.2 %all-gather.5.cloned.1.call-done = bf16[14336,128]{1,0:T(8,128)(2,1)} async-done(((bf16[1792,128]{1,0:T(8,128)(2,1)}), bf16[14336,128]{1,0:T(8,128)(2,1)}) %all-gather.5.cloned.1.call-update) | async-done | bytes 3670032 | tf_op jit(solution)/shard_map/all_gather | solution.py:59
  246.7 1.6 constant_dynamic-slice_fusion
  248.4 23.6 %select_reduce_fusion = f32[]{:T(128)} fusion(bf16[1792,7168]{1,0:T(8,128)(2,1)} %param.4, s32[1792]{0:T(1024)S(1)} %get-tuple-element.20), kind=kLoop, calls=%fused_computation | loop fusion | flops 51380224 | bytes 25697284 | tf_op jit(solution)/shard_map/reduce_sum | solution.py:50
  272.0 12.8 %convolution_bitcast_fusion = f32[1792,128]{1,0:T(8,128)} fusion(bf16[1792,7168]{1,0:T(8,128)(2,1)} %param.4, bf16[7168,128]{1,0:T(8,128)(2,1)S(1)} %collective-permute-done.2), kind=kOutput, calls=%fused_computation.4 | convolution fusion | flops 3288334336 | bytes 28442624 | tf_op jit(solution)/shard_map/dot_general | solution.py:66
  285.3 1.0 convolution_bitcast_fusion.4
  286.3 0.8 multiply_reduce_fusion
  288.3 66.2 %all-reduce.5.cloned.1.call-done = f32[128,128]{0,1:T(8,128)} async-done(((f32[128,128]{0,1:T(8,128)}), f32[128,128]{0,1:T(8,128)}) %all-reduce.5.cloned.1.call-update) | async-done | bytes 65552 | tf_op jit(solution)/shard_map/psum | solution.py:57
  354.5 1.2 fusion.9
  355.7 1.2 fusion.1
  357.0 14.0 %multiply_reduce_fusion.3 = (f32[]{:T(128)}, f32[]{:T(128)}, f32[]{:T(128)}, f32[1792,128]{1,0:T(8,128)}) fusion(f32[1792,128]{1,0:T(8,128)S(1)} %copy-done.3, f32[1792,128]{1,0:T(8,128)S(1)} %get-tuple-element.16, f32[1792,128]{1,0:T(8,128)S(1)} %fusion.1, f32[1792,128]{1,0:T(8,128)} %collective-permute-done.3, bf16[1792,7168]{1,0:T(8,128)(2,1)} %param.4, ...), kind=kOutput, calls=%fused_computation.19 | convolution fusion | flops 3290398720 | bytes 32112656 | tf_op jit(solution)/shard_map/dot_general | solution.py:65
  371.0 2.0 pad_maximum_fusion
  373.0 30.3 %psum.23 = f32[4]{0:T(128)S(1)} all-reduce(f32[4]{0:T(128)S(1)} %pad_maximum_fusion), channel_id=1, replica_groups=mesh['groups'=2,'row'=8,'col'=2] {'row','col'}, use_global_device_ids=true, to_apply=%region_7.8 | all-reduce | flops 4 | bytes 32 | tf_op jit(solution)/shard_map/psum | solution.py:78
  403.2 0.6 fusion.26
  410.2 3.2 multiply_subtract_fusion
  (30 shorter events, 1.1 us)
Async XLA Ops:
  6.5 74.1 %all-gather.3.cloned.1.call-start = ((), (), s32[]{:S(2)}) async-start(), calls=%async_computation | async-start | bytes 4128768 | tf_op jit(solution)/shard_map/all_gather | solution.py:59
  8.6 74.9 %copy-start = (bf16[128,1792]{1,0:T(8,128)(2,1)S(1)}, bf16[128,1792]{1,0:T(8,128)(2,1)}, u32[]{:S(2)}) copy-start(bf16[128,1792]{1,0:T(8,128)(2,1)} %param.5) | copy-start | bytes 1376260
  11.6 72.0 %copy-start.2 = (bf16[1792,128]{1,0:T(8,128)(2,1)S(1)}, bf16[1792,128]{1,0:T(8,128)(2,1)}, u32[]{:S(2)}) copy-start(bf16[1792,128]{1,0:T(8,128)(2,1)} %get-tuple-element.10) | copy-start | bytes 1376260
  11.6 141.2 %all-reduce.3.cloned.1.call-start = ((), (), s32[]{:S(2)}) async-start(), calls=%async_computation.1 | async-start | bytes 131072 | tf_op jit(solution)/shard_map/psum | solution.py:57
  83.5 70.4 %collective-permute-start = (bf16[7168,128]{1,0:T(8,128)(2,1)}, bf16[7168,128]{1,0:T(8,128)(2,1)}, u32[]{:S(2)}, u32[]{:S(2)}) collective-permute-start(bf16[7168,128]{1,0:T(8,128)(2,1)} %constant_dynamic-slice_fusion.1), channel_id=1, source_target_pairs={{0,1},{1,0},{2,3},{3,2},{4,5},{5,4},{6,7},{7,6},{8,9},{9,8},{10,11... | collective-permute-start | bytes 5505032 | tf_op jit(solution)/shard_map/ppermute | solution.py:13
  84.5 162.2 %all-gather.5.cloned.1.call-start = ((), (), s32[]{:S(2)}) async-start(), calls=%async_computation.2 | async-start | bytes 4128768 | tf_op jit(solution)/shard_map/all_gather | solution.py:59
  153.9 12.6 %copy-start.4 = (bf16[14336,128]{1,0:T(8,128)(2,1)S(1)}, bf16[14336,128]{1,0:T(8,128)(2,1)}, u32[]{:S(2)}) copy-start(bf16[14336,128]{1,0:T(8,128)(2,1)} %all-gather.3.cloned.1.call-done) | copy-start | bytes 11010052
  166.4 11.9 %copy-start.5 = (f32[128,128]{0,1:T(8,128)S(1)}, f32[128,128]{0,1:T(8,128)}, u32[]{:S(2)}) copy-start(f32[128,128]{0,1:T(8,128)} %all-reduce.3.cloned.1.call-done) | copy-start | bytes 196612
  166.5 11.9 %collective-permute-start.1 = (f32[1792,128]{1,0:T(8,128)S(1)}, f32[1792,128]{1,0:T(8,128)S(1)}, u32[]{:S(2)}, u32[]{:S(2)}) collective-permute-start(f32[1792,128]{1,0:T(8,128)S(1)} %convolution_bitcast_fusion.2), channel_id=1, source_target_pairs={{0,1},{1,0},{2,3},{3,2},{4,5},{5,4},{6,7},{7,6},{8,9},{9,8},{10,11... | collective-permute-start | bytes 2752520 | tf_op jit(solution)/shard_map/ppermute | solution.py:13
  180.2 174.2 %all-reduce.5.cloned.1.call-start = ((), (), s32[]{:S(2)}) async-start(), calls=%async_computation.3 | async-start | bytes 131072 | tf_op jit(solution)/shard_map/psum | solution.py:57
  248.3 23.7 %collective-permute-start.2 = (bf16[7168,128]{1,0:T(8,128)(2,1)S(1)}, bf16[7168,128]{1,0:T(8,128)(2,1)S(1)}, u32[]{:S(2)}, u32[]{:S(2)}) collective-permute-start(bf16[7168,128]{1,0:T(8,128)(2,1)S(1)} %constant_dynamic-slice_fusion), channel_id=1, source_target_pairs={{0,1},{1,0},{2,3},{3,2},{4,5},{5,4},{6,7},{7,6},{8,9},{9,8},{10,11... | collective-permute-start | bytes 5505032 | tf_op jit(solution)/shard_map/ppermute | solution.py:13
  272.0 13.3 %copy-start.1 = (bf16[1792,128]{1,0:T(8,128)(2,1)S(1)}, bf16[1792,128]{1,0:T(8,128)(2,1)}, u32[]{:S(2)}) copy-start(bf16[1792,128]{1,0:T(8,128)(2,1)} %get-tuple-element.8) | copy-start | bytes 1376260
  284.8 72.2 %collective-permute-start.3 = (f32[1792,128]{1,0:T(8,128)}, f32[1792,128]{1,0:T(8,128)}, u32[]{:S(2)}, u32[]{:S(2)}) collective-permute-start(f32[1792,128]{1,0:T(8,128)} %convolution_bitcast_fusion), channel_id=1, source_target_pairs={{0,1},{1,0},{2,3},{3,2},{4,5},{5,4},{6,7},{7,6},{8,9},{9,8},{10,11... | collective-permute-start | bytes 2752520 | tf_op jit(solution)/shard_map/ppermute | solution.py:13
  354.5 2.5 copy-start.3
Sparse Core Ops, SparseCore 0:
  11.7 68.9 all-gather.2
  84.6 68.1 all-reduce.2
  180.4 66.2 all-gather.4
  286.4 68.0 all-reduce.4
where the time goes:
time: 420 us
  waiting for transfers between devices  270 us (64%)
  matrix products  63.5 us (15%)
  blocking collectives  30.3 us (7%)
  other arithmetic  29.6 us (7%)
  between operations  20.8 us (5%)
  local copies, waits for them, and re-layouts  5.13 us (1%)
    all_gather x2, waiting for transfers between devices, apply_gram(): column_panel = lax.all_gather(panel_low, 'row', axis=0, tiled=True)  135 us
    psum x2, waiting for transfers between devices, apply_gram(): lax.psum(jnp.dot(activations, panel_low, preferred_element_type=jnp.float...  134 us
    psum x1, blocking collectives, per_device(): lax.psum(jnp.stack([local_square, local_curve, local_curve_square, trace_...  30.3 us
    dot_general x2, matrix products, apply_gram(): own_part = jnp.dot(gram_old, own_half, preferred_element_type=jnp.float32)  25.8 us
    dot_general x2, matrix products, apply_gram(): jnp.dot(gram_old, partner_half, preferred_element_type=jnp.float32)  25.3 us
    reduce_sum x1, other arithmetic, per_device(): jnp.sum(jnp.where(on_diagonal, gram_old.astype(jnp.float32), 0.0))  23.6 us
  transfers between devices with their start and end apart: 8, of which 4 were waited for; matrix products, arithmetic and copies ran while one was open for 10% of the time, Pallas kernels for 0%

commit v1 on v0

--- a/solution.py
+++ b/solution.py
@@ -56,7 +56,29 @@
         panel_low = panel.astype(jnp.bfloat16)
         inner = lax.psum(jnp.dot(activations, panel_low, preferred_element_type=jnp.float32), "row")
         low_rank = update_product(activations, inner)
-        column_panel = lax.all_gather(panel_low, "row", axis=0, tiled=True)
+        response = lax.psum(1, "row")
+        inter = lax.axis_index("row")
+        then, value_now, before = (response, inter, panel_low.shape[0])
+        buffer = [(k0, (k0 + 1) % then) for k0 in range(then)]
+        column_panel = jnp.zeros(
+            (*panel_low.shape[:0], then * before, *panel_low.shape[0 + 1 :]), panel_low.dtype
+        )
+        items = [(k0, (k0 - 1) % then) for k0 in range(then)]
+        fresh = b_now = panel_low
+        shaped = then // 2
+        column_panel = lax.dynamic_update_slice_in_dim(
+            column_panel, panel_low, value_now * before, axis=0
+        )
+        for dd in range(1, shaped + 1):
+            fresh = lax.ppermute(fresh, "row", buffer)
+            column_panel = lax.dynamic_update_slice_in_dim(
+                column_panel, fresh, (value_now - dd) % then * before, axis=0
+            )
+            if dd < then - shaped:
+                b_now = lax.ppermute(b_now, "row", items)
+                column_panel = lax.dynamic_update_slice_in_dim(
+                    column_panel, b_now, (value_now + dd) % then * before, axis=0
+                )
         own_half = lax.dynamic_slice_in_dim(column_panel, half_offset, half_width, 0)
         partner_need = lax.dynamic_slice_in_dim(
             column_panel, (1 - col_index) * half_width, half_width, 0

time: 420 us -> 450 us (1.071)
  starting transfers between devices: 0.94 us -> 23.6 us
  local copies, waits for them, and re-layouts: 5.13 us -> 12 us
    all_gather x2 -> x0, waiting for transfers between devices: 135 us -> none  [apply_gram(): column_panel = lax.all_gather(panel_low, 'row', axis=0, tiled=True)]
    ppermute x0 -> x14, waiting for transfers between devices: none -> 133 us  [the longest x8 79.3 us: apply_gram(): fresh = lax.ppermute(fresh, 'row', buffer)]
    ppermute x0 -> x14, starting transfers between devices: none -> 23.3 us  [the longest x6 15.9 us: apply_gram(): b_now = lax.ppermute(b_now, 'row', items)]
    dynamic_update_slice x0 -> x14, local copies, waits for them, and re-layouts: none -> 6.12 us  [the longest x8 3.5 us: apply_gram(): lax.dynamic_update_slice_in_dim(column_panel, fresh, (value_now - dd) % t...]
  transfers between devices with their start and end apart: 8 -> 20, of which waited for: 4 -> 13; matrix products, arithmetic and copies ran while one was open for 10% -> 8% of each run, Pallas kernels for 0% -> 0%
where the time goes in v1:
time: 450 us
  waiting for transfers between devices  270 us (60%)
  matrix products  62.8 us (14%)
  blocking collectives  30.3 us (7%)
  other arithmetic  30.1 us (7%)
  starting transfers between devices  23.6 us (5%)
  between operations  21.2 us (5%)
  local copies, waits for them, and re-layouts  12 us (3%)
    psum x2, waiting for transfers between devices, apply_gram(): lax.psum(jnp.dot(activations, panel_low, preferred_element_type=jnp.float...  133 us
    ppermute x8, waiting for transfers between devices, apply_gram(): fresh = lax.ppermute(fresh, 'row', buffer)  79.3 us
    ppermute x6, waiting for transfers between devices, apply_gram(): b_now = lax.ppermute(b_now, 'row', items)  54.1 us
    psum x1, blocking collectives, per_device(): lax.psum(jnp.stack([local_square, local_curve, local_curve_square, trace_...  30.3 us
    dot_general x2, matrix products, apply_gram(): own_part = jnp.dot(gram_old, own_half, preferred_element_type=jnp.float32)  26.6 us
    dot_general x2, matrix products, apply_gram(): jnp.dot(gram_old, partner_half, preferred_element_type=jnp.float32)  25.5 us
    reduce_sum x1, other arithmetic, per_device(): jnp.sum(jnp.where(on_diagonal, gram_old.astype(jnp.float32), 0.0))  24.7 us
    ppermute x6, starting transfers between devices, apply_gram(): b_now = lax.ppermute(b_now, 'row', items)  15.9 us
  transfers between devices with their start and end apart: 20, of which 13 were waited for; matrix products, arithmetic and copies ran while one was open for 8% of the time, Pallas kernels for 0%

profile of v1, /device:TPU:0, one launch (start us, length us, event | category | flops | bytes accessed | tf_op | source)
XLA Modules:
  0.0 449.7 jit_solution(15256558612352415458)
XLA Ops:
  12.4 6.0 %collective-permute-start.1 = (bf16[1792,128]{1,0:T(8,128)(2,1)S(1)}, bf16[1792,128]{1,0:T(8,128)(2,1)S(1)}, u32[]{:S(2)}, u32[]{:S(2)}) collective-permute-start(bf16[1792,128]{1,0:T(8,128)(2,1)S(1)} %get-tuple-element.12), channel_id=1, source_target_pairs={{0,14},{2,0},{4,2},{6,4},{8,6},{10,8},{12,10},{14,12},{1,15},{3,1}... | collective-permute-start | bytes 1376264 | tf_op jit(solution)/shard_map/ppermute | solution.py:78
  18.5 17.3 %collective-permute-done.1 = bf16[1792,128]{1,0:T(8,128)(2,1)S(1)} collective-permute-done((bf16[1792,128]{1,0:T(8,128)(2,1)S(1)}, bf16[1792,128]{1,0:T(8,128)(2,1)S(1)}, u32[]{:S(2)}, u32[]{:S(2)}) %collective-permute-start.1) | collective-permute-done | bytes 458784 | tf_op jit(solution)/shard_map/ppermute | solution.py:78
  35.8 2.8 collective-permute-start.3
  40.2 17.0 %collective-permute-done.3 = bf16[1792,128]{1,0:T(8,128)(2,1)S(1)} collective-permute-done((bf16[1792,128]{1,0:T(8,128)(2,1)S(1)}, bf16[1792,128]{1,0:T(8,128)(2,1)S(1)}, u32[]{:S(2)}, u32[]{:S(2)}) %collective-permute-start.3) | collective-permute-done | bytes 458784 | tf_op jit(solution)/shard_map/ppermute | solution.py:78
  57.3 2.6 collective-permute-start.5
  61.5 15.3 %collective-permute-done.4 = bf16[1792,128]{1,0:T(8,128)(2,1)S(1)} collective-permute-done((bf16[1792,128]{1,0:T(8,128)(2,1)S(1)}, bf16[1792,128]{1,0:T(8,128)(2,1)S(1)}, u32[]{:S(2)}, u32[]{:S(2)}) %collective-permute-start.4) | collective-permute-done | bytes 458784 | tf_op jit(solution)/shard_map/ppermute | solution.py:73
  80.9 13.6 %collective-permute-done.6 = bf16[1792,128]{1,0:T(8,128)(2,1)S(1)} collective-permute-done((bf16[1792,128]{1,0:T(8,128)(2,1)S(1)}, bf16[1792,128]{1,0:T(8,128)(2,1)S(1)}, u32[]{:S(2)}, u32[]{:S(2)}) %collective-permute-start.6) | collective-permute-done | bytes 458784 | tf_op jit(solution)/shard_map/ppermute | solution.py:73
  97.0 3.8 collective-permute-done.7
  100.7 12.8 %convolution_bitcast_fusion.2 = f32[1792,128]{1,0:T(8,128)} fusion(bf16[1792,7168]{1,0:T(8,128)(2,1)} %param.4, bf16[7168,128]{1,0:T(8,128)(2,1)S(1)} %collective-permute-done.7), kind=kOutput, calls=%fused_computation.6 | convolution fusion | flops 3288334336 | bytes 28442624 | tf_op jit(solution)/shard_map/dot_general | solution.py:88
  114.7 67.9 %all-reduce.3.cloned.1.call-done = f32[128,128]{0,1:T(8,128)} async-done(((f32[128,128]{0,1:T(8,128)}), f32[128,128]{0,1:T(8,128)}) %all-reduce.3.cloned.1.call-update) | async-done | bytes 65552 | tf_op jit(solution)/shard_map/psum | solution.py:57
  186.4 12.6 %constant_dynamic-update-slice_fusion.7 = (bf16[14336,128]{1,0:T(8,128)(2,1)S(1)}, bf16[1792,128]{1,0:T(8,128)(2,1)S(1)}, f32[1792,128]{1,0:T(8,128)S(1)}, f32[1792,128]{1,0:T(8,128)S(1)}) fusion(bf16[14336,128]{1,0:T(8,128)(2,1)S(1)} %broadcast.97, s32[]{:T(128)S(6)} %select_n.109, f32[1792,128]{1,0:T(8,128)S(1)} %get-tuple-element.18, ...), kind=kOutput, calls=%fused_computation.57 | convolution fusion | flops 3289251840 | bytes 33030152 | tf_op jit(solution)/shard_map/dot_general | solution.py:87
  199.1 3.3 collective-permute-start.10
  202.4 17.2 %collective-permute-done.10 = bf16[1792,128]{1,0:T(8,128)(2,1)S(1)} collective-permute-done((bf16[1792,128]{1,0:T(8,128)(2,1)S(1)}, bf16[1792,128]{1,0:T(8,128)(2,1)S(1)}, u32[]{:S(2)}, u32[]{:S(2)}) %collective-permute-start.10) | collective-permute-done | bytes 458784 | tf_op jit(solution)/shard_map/ppermute | solution.py:78
  220.7 8.4 %collective-permute-done.9 = bf16[1792,128]{1,0:T(8,128)(2,1)S(1)} collective-permute-done((bf16[1792,128]{1,0:T(8,128)(2,1)S(1)}, bf16[1792,128]{1,0:T(8,128)(2,1)S(1)}, u32[]{:S(2)}, u32[]{:S(2)}) %collective-permute-start.9) | collective-permute-done | bytes 458784 | tf_op jit(solution)/shard_map/ppermute | solution.py:73
  231.7 2.5 collective-permute-done.12
  234.2 17.2 %collective-permute-done.11 = bf16[1792,128]{1,0:T(8,128)(2,1)S(1)} collective-permute-done((bf16[1792,128]{1,0:T(8,128)(2,1)S(1)}, bf16[1792,128]{1,0:T(8,128)(2,1)S(1)}, u32[]{:S(2)}, u32[]{:S(2)}) %collective-permute-start.11) | collective-permute-done | bytes 458784 | tf_op jit(solution)/shard_map/ppermute | solution.py:73
  253.9 11.7 %collective-permute-done.13 = bf16[1792,128]{1,0:T(8,128)(2,1)S(1)} collective-permute-done((bf16[1792,128]{1,0:T(8,128)(2,1)S(1)}, bf16[1792,128]{1,0:T(8,128)(2,1)S(1)}, u32[]{:S(2)}, u32[]{:S(2)}) %collective-permute-start.13) | collective-permute-done | bytes 458784 | tf_op jit(solution)/shard_map/ppermute | solution.py:73
  265.7 13.3 %collective-permute-done.15 = bf16[1792,128]{1,0:T(8,128)(2,1)S(1)} collective-permute-done((bf16[1792,128]{1,0:T(8,128)(2,1)S(1)}, bf16[1792,128]{1,0:T(8,128)(2,1)S(1)}, u32[]{:S(2)}, u32[]{:S(2)}) %collective-permute-start.15) | collective-permute-done | bytes 458784 | tf_op jit(solution)/shard_map/ppermute | solution.py:73
  279.3 24.7 %select_reduce_fusion = f32[]{:T(128)} fusion(bf16[1792,7168]{1,0:T(8,128)(2,1)} %param.4, s32[1792]{0:T(1024)S(1)} %get-tuple-element.22), kind=kLoop, calls=%fused_computation | loop fusion | flops 51380224 | bytes 25697284 | tf_op jit(solution)/shard_map/reduce_sum | solution.py:50
  304.0 12.8 %convolution_bitcast_fusion = f32[1792,128]{1,0:T(8,128)} fusion(bf16[1792,7168]{1,0:T(8,128)(2,1)} %param.4, bf16[7168,128]{1,0:T(8,128)(2,1)S(1)} %collective-permute-done.16), kind=kOutput, calls=%fused_computation.4 | convolution fusion | flops 3288334336 | bytes 28442624 | tf_op jit(solution)/shard_map/dot_general | solution.py:88
  319.9 64.7 %all-reduce.5.cloned.1.call-done = f32[128,128]{0,1:T(8,128)} async-done(((f32[128,128]{0,1:T(8,128)}), f32[128,128]{0,1:T(8,128)}) %all-reduce.5.cloned.1.call-update) | async-done | bytes 65552 | tf_op jit(solution)/shard_map/psum | solution.py:57
  387.2 14.0 %multiply_reduce_fusion.3 = (f32[]{:T(128)}, f32[]{:T(128)}, f32[]{:T(128)}, f32[1792,128]{1,0:T(8,128)}) fusion(f32[1792,128]{1,0:T(8,128)S(1)} %get-tuple-element.10, f32[1792,128]{1,0:T(8,128)S(1)} %get-tuple-element.18, f32[1792,128]{1,0:T(8,128)S(1)} %fusion.1, f32[1792,128]{1,0:T(8,128)} %collective-permute-done.17, bf16[1792,7168]{1,0:T(8,128)(2,1)} %param.4, ...), kind=kOutput, calls=%fused_computation.22 | convolution fusion | flops 3290398720 | bytes 32112656 | tf_op jit(solution)/shard_map/dot_general | solution.py:87
  403.0 30.3 %psum.23 = f32[4]{0:T(128)S(1)} all-reduce(f32[4]{0:T(128)S(1)} %pad_maximum_fusion), channel_id=1, replica_groups=mesh['groups'=2,'row'=8,'col'=2] {'row','col'}, use_global_device_ids=true, to_apply=%region_7.8 | all-reduce | flops 4 | bytes 32 | tf_op jit(solution)/shard_map/psum | solution.py:100
  440.3 2.6 multiply_subtract_fusion
  (66 shorter events, 34.4 us)
Async XLA Ops:
  6.5 4.2 copy-start.4
  6.5 176.0 %all-reduce.3.cloned.1.call-start = ((), (), s32[]{:S(2)}) async-start(), calls=%async_computation | async-start | bytes 131072 | tf_op jit(solution)/shard_map/psum | solution.py:57
  12.4 23.3 %collective-permute-start.1 = (bf16[1792,128]{1,0:T(8,128)(2,1)S(1)}, bf16[1792,128]{1,0:T(8,128)(2,1)S(1)}, u32[]{:S(2)}, u32[]{:S(2)}) collective-permute-start(bf16[1792,128]{1,0:T(8,128)(2,1)S(1)} %get-tuple-element.12), channel_id=1, source_target_pairs={{0,14},{2,0},{4,2},{6,4},{8,6},{10,8},{12,10},{14,12},{1,15},{3,1}... | collective-permute-start | bytes 1376264 | tf_op jit(solution)/shard_map/ppermute | solution.py:78
  18.5 20.1 %collective-permute-start = (bf16[1792,128]{1,0:T(8,128)(2,1)S(1)}, bf16[1792,128]{1,0:T(8,128)(2,1)S(1)}, u32[]{:S(2)}, u32[]{:S(2)}) collective-permute-start(bf16[1792,128]{1,0:T(8,128)(2,1)S(1)} %get-tuple-element.12), channel_id=1, source_target_pairs={{0,2},{2,4},{4,6},{6,8},{8,10},{10,12},{12,14},{14,0},{1,3},{3,5},... | collective-permute-start | bytes 1376264 | tf_op jit(solution)/shard_map/ppermute | solution.py:73
  35.8 21.5 %collective-permute-start.3 = (bf16[1792,128]{1,0:T(8,128)(2,1)S(1)}, bf16[1792,128]{1,0:T(8,128)(2,1)S(1)}, u32[]{:S(2)}, u32[]{:S(2)}) collective-permute-start(bf16[1792,128]{1,0:T(8,128)(2,1)S(1)} %collective-permute-done.1), channel_id=1, source_target_pairs={{0,14},{2,0},{4,2},{6,4},{8,6},{10,8},{12,10},{14,12},{1,15},{3,1}... | collective-permute-start | bytes 1376264 | tf_op jit(solution)/shard_map/ppermute | solution.py:78
  38.6 21.2 %collective-permute-start.2 = (bf16[1792,128]{1,0:T(8,128)(2,1)S(1)}, bf16[1792,128]{1,0:T(8,128)(2,1)S(1)}, u32[]{:S(2)}, u32[]{:S(2)}) collective-permute-start(bf16[1792,128]{1,0:T(8,128)(2,1)S(1)} %collective-permute-done), channel_id=1, source_target_pairs={{0,2},{2,4},{4,6},{6,8},{8,10},{10,12},{12,14},{14,0},{1,3},{3,5},... | collective-permute-start | bytes 1376264 | tf_op jit(solution)/shard_map/ppermute | solution.py:73
  57.3 22.8 %collective-permute-start.5 = (bf16[1792,128]{1,0:T(8,128)(2,1)S(1)}, bf16[1792,128]{1,0:T(8,128)(2,1)S(1)}, u32[]{:S(2)}, u32[]{:S(2)}) collective-permute-start(bf16[1792,128]{1,0:T(8,128)(2,1)S(1)} %collective-permute-done.3), channel_id=1, source_target_pairs={{0,14},{2,0},{4,2},{6,4},{8,6},{10,8},{12,10},{14,12},{1,15},{3,1}... | collective-permute-start | bytes 1376264 | tf_op jit(solution)/shard_map/ppermute | solution.py:78
  59.8 16.9 %collective-permute-start.4 = (bf16[1792,128]{1,0:T(8,128)(2,1)S(1)}, bf16[1792,128]{1,0:T(8,128)(2,1)S(1)}, u32[]{:S(2)}, u32[]{:S(2)}) collective-permute-start(bf16[1792,128]{1,0:T(8,128)(2,1)S(1)} %collective-permute-done.2), channel_id=1, source_target_pairs={{0,2},{2,4},{4,6},{6,8},{8,10},{10,12},{12,14},{14,0},{1,3},{3,5},... | collective-permute-start | bytes 1376264 | tf_op jit(solution)/shard_map/ppermute | solution.py:73
  76.8 17.7 %collective-permute-start.6 = (bf16[1792,128]{1,0:T(8,128)(2,1)S(1)}, bf16[1792,128]{1,0:T(8,128)(2,1)S(1)}, u32[]{:S(2)}, u32[]{:S(2)}) collective-permute-start(bf16[1792,128]{1,0:T(8,128)(2,1)S(1)} %collective-permute-done.4), channel_id=1, source_target_pairs={{0,2},{2,4},{4,6},{6,8},{8,10},{10,12},{12,14},{14,0},{1,3},{3,5},... | collective-permute-start | bytes 1376264 | tf_op jit(solution)/shard_map/ppermute | solution.py:73
  96.9 16.8 %copy-start = (bf16[128,1792]{1,0:T(8,128)(2,1)S(1)}, bf16[128,1792]{1,0:T(8,128)(2,1)}, u32[]{:S(2)}) copy-start(bf16[128,1792]{1,0:T(8,128)(2,1)} %param.5) | copy-start | bytes 1376260
  96.9 3.9 collective-permute-start.7
  113.5 71.5 %collective-permute-start.8 = (f32[1792,128]{1,0:T(8,128)}, f32[1792,128]{1,0:T(8,128)S(1)}, u32[]{:S(2)}, u32[]{:S(2)}) collective-permute-start(f32[1792,128]{1,0:T(8,128)} %convolution_bitcast_fusion.2), channel_id=1, source_target_pairs={{0,1},{1,0},{2,3},{3,2},{4,5},{5,4},{6,7},{7,6},{8,9},{9,8},{10,11... | collective-permute-start | bytes 2752520 | tf_op jit(solution)/shard_map/ppermute | solution.py:13
  114.6 269.9 %all-reduce.5.cloned.1.call-start = ((), (), s32[]{:S(2)}) async-start(), calls=%async_computation.1 | async-start | bytes 131072 | tf_op jit(solution)/shard_map/psum | solution.py:57
  199.1 20.6 %collective-permute-start.10 = (bf16[1792,128]{1,0:T(8,128)(2,1)S(1)}, bf16[1792,128]{1,0:T(8,128)(2,1)S(1)}, u32[]{:S(2)}, u32[]{:S(2)}) collective-permute-start(bf16[1792,128]{1,0:T(8,128)(2,1)S(1)} %get-tuple-element.9), channel_id=1, source_target_pairs={{0,14},{2,0},{4,2},{6,4},{8,6},{10,8},{12,10},{14,12},{1,15},{3,1}... | collective-permute-start | bytes 1376264 | tf_op jit(solution)/shard_map/ppermute | solution.py:78
  202.4 26.7 %collective-permute-start.9 = (bf16[1792,128]{1,0:T(8,128)(2,1)S(1)}, bf16[1792,128]{1,0:T(8,128)(2,1)S(1)}, u32[]{:S(2)}, u32[]{:S(2)}) collective-permute-start(bf16[1792,128]{1,0:T(8,128)(2,1)S(1)} %get-tuple-element.9), channel_id=1, source_target_pairs={{0,2},{2,4},{4,6},{6,8},{8,10},{10,12},{12,14},{14,0},{1,3},{3,5},... | collective-permute-start | bytes 1376264 | tf_op jit(solution)/shard_map/ppermute | solution.py:73
  219.6 14.5 %collective-permute-start.12 = (bf16[1792,128]{1,0:T(8,128)(2,1)S(1)}, bf16[1792,128]{1,0:T(8,128)(2,1)S(1)}, u32[]{:S(2)}, u32[]{:S(2)}) collective-permute-start(bf16[1792,128]{1,0:T(8,128)(2,1)S(1)} %collective-permute-done.10), channel_id=1, source_target_pairs={{0,14},{2,0},{4,2},{6,4},{8,6},{10,8},{12,10},{14,12},{1,15},{3,1}... | collective-permute-start | bytes 1376264 | tf_op jit(solution)/shard_map/ppermute | solution.py:78
  229.1 22.2 %collective-permute-start.11 = (bf16[1792,128]{1,0:T(8,128)(2,1)S(1)}, bf16[1792,128]{1,0:T(8,128)(2,1)S(1)}, u32[]{:S(2)}, u32[]{:S(2)}) collective-permute-start(bf16[1792,128]{1,0:T(8,128)(2,1)S(1)} %collective-permute-done.9), channel_id=1, source_target_pairs={{0,2},{2,4},{4,6},{6,8},{8,10},{10,12},{12,14},{14,0},{1,3},{3,5},... | collective-permute-start | bytes 1376264 | tf_op jit(solution)/shard_map/ppermute | solution.py:73
  234.2 31.5 %collective-permute-start.14 = (bf16[1792,128]{1,0:T(8,128)(2,1)S(1)}, bf16[1792,128]{1,0:T(8,128)(2,1)S(1)}, u32[]{:S(2)}, u32[]{:S(2)}) collective-permute-start(bf16[1792,128]{1,0:T(8,128)(2,1)S(1)} %collective-permute-done.12), channel_id=1, source_target_pairs={{0,14},{2,0},{4,2},{6,4},{8,6},{10,8},{12,10},{14,12},{1,15},{3,1}... | collective-permute-start | bytes 1376264 | tf_op jit(solution)/shard_map/ppermute | solution.py:78
  251.3 14.3 %collective-permute-start.13 = (bf16[1792,128]{1,0:T(8,128)(2,1)S(1)}, bf16[1792,128]{1,0:T(8,128)(2,1)S(1)}, u32[]{:S(2)}, u32[]{:S(2)}) collective-permute-start(bf16[1792,128]{1,0:T(8,128)(2,1)S(1)} %collective-permute-done.11), channel_id=1, source_target_pairs={{0,2},{2,4},{4,6},{6,8},{8,10},{10,12},{12,14},{14,0},{1,3},{3,5},... | collective-permute-start | bytes 1376264 | tf_op jit(solution)/shard_map/ppermute | solution.py:73
  265.6 13.4 %collective-permute-start.15 = (bf16[1792,128]{1,0:T(8,128)(2,1)S(1)}, bf16[1792,128]{1,0:T(8,128)(2,1)S(1)}, u32[]{:S(2)}, u32[]{:S(2)}) collective-permute-start(bf16[1792,128]{1,0:T(8,128)(2,1)S(1)} %collective-permute-done.13), channel_id=1, source_target_pairs={{0,2},{2,4},{4,6},{6,8},{8,10},{10,12},{12,14},{14,0},{1,3},{3,5},... | collective-permute-start | bytes 1376264 | tf_op jit(solution)/shard_map/ppermute | solution.py:73
  279.1 24.9 %copy-start.1 = (bf16[14336,128]{1,0:T(8,128)(2,1)}, bf16[14336,128]{1,0:T(8,128)(2,1)S(1)}, u32[]{:S(2)}) copy-start(bf16[14336,128]{1,0:T(8,128)(2,1)S(1)} %constant_dynamic-update-slice_fusion) | copy-start | bytes 11010052
  279.2 24.7 %collective-permute-start.16 = (bf16[7168,128]{1,0:T(8,128)(2,1)S(1)}, bf16[7168,128]{1,0:T(8,128)(2,1)S(1)}, u32[]{:S(2)}, u32[]{:S(2)}) collective-permute-start(bf16[7168,128]{1,0:T(8,128)(2,1)S(1)} %constant_dynamic-slice_fusion), channel_id=1, source_target_pairs={{0,1},{1,0},{2,3},{3,2},{4,5},{5,4},{6,7},{7,6},{8,9},{9,8},{10,11... | collective-permute-start | bytes 5505032 | tf_op jit(solution)/shard_map/ppermute | solution.py:13
  316.7 70.4 %collective-permute-start.17 = (f32[1792,128]{1,0:T(8,128)}, f32[1792,128]{1,0:T(8,128)}, u32[]{:S(2)}, u32[]{:S(2)}) collective-permute-start(f32[1792,128]{1,0:T(8,128)} %convolution_bitcast_fusion), channel_id=1, source_target_pairs={{0,1},{1,0},{2,3},{3,2},{4,5},{5,4},{6,7},{7,6},{8,9},{9,8},{10,11... | collective-permute-start | bytes 2752520 | tf_op jit(solution)/shard_map/ppermute | solution.py:13
  384.6 2.6 copy-start.2
  (1 other events, 0.9 us)
Sparse Core Ops, SparseCore 0:
  114.7 67.7 all-reduce.2
  317.9 66.6 all-reduce.4
